TPU v7x, 32 devices: a whole 2x2x4 slice. The times are simulated.
32 devices in a mesh: feat: 8 (over z, y), tok: 4 (over x, core).
Axes of the slice: x: 2, y: 2, z: 4, core: 2. Of those that a mesh axis runs over, the one named last changes fastest.
Arguments:
- activations: bfloat16 [2048, 7168], P('tok', 'feat'), may hold values from -6 to 6
- top_lists: int32 [2048, 64], P('tok'), may hold values from 0 to 4095, all different within a row
- encoder_weight: bfloat16 [7168, 4096], P(None, 'feat'), may hold values from -0.0625 to 0.0625
- encoder_bias: float32 [4096], P('feat'), may hold values from -3 to 3
- decoder_weight: bfloat16 [7168, 4096], P(None, 'feat'), may hold values from -0.125 to 0.125
- decoder_bias: float32 [7168], replicated, may hold values from -3 to 3
Outputs:
- encoder_grad: float32 [7168, 4096], P('tok', 'feat')
- decoder_grad: float32 [7168, 4096], P('tok', 'feat')
All inputs are finite; a program needn't handle non-finite values.
Results may differ from a plain program's by a relative error of at most 0.004.
Values may be sent and summed in bfloat16 or wider, within the bound.
A program may use at most 128 MiB of HBM per device.

v0:
```python
import jax
import jax.numpy as jnp
from jax import lax
from jax.sharding import PartitionSpec as P


def contract_rows(left, right):
    return lax.dot_general(
        left, right, (((0,), (0,)), ((), ())), preferred_element_type=jnp.float32
    )


def body(activations, top_lists, encoder_weight, encoder_bias, decoder_weight, decoder_bias):
    group_rows = activations.shape[0]
    feat_dev = encoder_weight.shape[1]
    shards = lax.axis_size("feat")
    owner = lax.axis_index("feat")
    row_share = group_rows // shards
    gathered = lax.all_gather(activations, "feat", axis=1, tiled=True)
    encoded = jnp.dot(gathered, encoder_weight, preferred_element_type=jnp.float32) + encoder_bias
    local_ids = top_lists - owner * feat_dev
    inside = (local_ids >= 0) & (local_ids < feat_dev)
    column = jnp.where(inside, local_ids, feat_dev)
    row_ids = jnp.arange(group_rows, dtype=jnp.int32)[:, None]
    chosen = (
        jnp.zeros((group_rows, feat_dev), jnp.float32).at[row_ids, column].set(1.0, mode="drop")
    )
    codes = jnp.where(chosen > 0.0, encoded, 0.0).astype(jnp.bfloat16)
    rebuilt = lax.psum_scatter(
        lax.dot_general(
            codes, decoder_weight, (((1,), (1,)), ((), ())), preferred_element_type=jnp.float32
        ),
        "feat",
        scatter_dimension=0,
        tiled=True,
    )
    own_rows = lax.dynamic_slice_in_dim(gathered, owner * row_share, row_share, 0)
    error_rows = (rebuilt + decoder_bias - own_rows.astype(jnp.float32)).astype(jnp.bfloat16)
    error = lax.all_gather(error_rows, "feat", axis=0, tiled=True)
    pulled = jnp.dot(error, decoder_weight, preferred_element_type=jnp.float32)
    code_grads = jnp.where(chosen > 0.0, pulled, 0.0).astype(jnp.bfloat16)
    input_cols, error_cols = (
        lax.all_to_all(gathered, "tok", split_axis=1, concat_axis=0, tiled=True),
        lax.all_to_all(error, "tok", split_axis=1, concat_axis=0, tiled=True),
    )
    grads_all, codes_all = (
        lax.all_gather(code_grads, "tok", axis=0, tiled=True),
        lax.all_gather(codes, "tok", axis=0, tiled=True),
    )
    encoder_grad = contract_rows(input_cols, grads_all)
    decoder_grad = contract_rows(error_cols, codes_all)
    return (encoder_grad, decoder_grad)


def solution(mesh):
    return jax.shard_map(
        body,
        mesh=mesh,
        in_specs=(
            P("tok", "feat"),
            P("tok", None),
            P(None, "feat"),
            P("feat"),
            P(None, "feat"),
            P(),
        ),
        out_specs=(P("tok", "feat"), P("tok", "feat")),
        check_vma=False,
    )
```

profile of v0, /device:TPU:0, one launch (start us, length us, event | category | flops | bytes accessed | tf_op | source)
XLA Modules:
  0.0 639.1 jit_solution(12103646338569349608)
XLA Ops:
  7.2 0.0 all-gather.5.cloned.1.call-start
  7.2 0.7 all-gather.5.cloned.1.call-update
  7.9 0.0 reduce-scatter.2.cloned.1.call-start
  7.9 0.9 fusion.5
  8.9 0.1 and_reduce_fusion
  9.0 0.8 multiply_reduce_fusion
  9.8 0.1 copy.12
  9.9 0.1 reshape.20
  10.0 120.3 %scatter_custom_fusion = f32[262144]{0:T(1024)S(1)} fusion(s32[32768]{0:T(1024)S(1)} %reshape.20, f32[32768]{0:T(1024)S(1)} %broadcast.30, f32[]{:T(128)} %constant.7.clone.1), kind=kCustom, calls=%fused_computation.11 | custom fusion | bytes 1048580
  130.3 0.1 broadcast_compare_fusion
  130.5 0.4 reshape.19
  130.8 0.0 all-gather.5.cloned.1.call-done
  130.9 9.1 %fusion.1 = bf16[512,512]{1,0:T(8,128)(2,1)S(1)} fusion(pred[512,512]{1,0:T(32,128)(4,1)S(1)} %reshape.19, bf16[512,7168]{1,0:T(8,128)(2,1)} %all-gather.5.cloned.1.call-done, bf16[7168,512]{1,0:T(8,128)(2,1)} %param.8, f32[512]{0:T(512)} %param.9), kind=kOutput, calls=%fused_computation.8 | convolution fusion | flops 3758882816 | bytes 15468544 | tf_op jit(solution)/shard_map/dot_general | solution.py:20
  140.0 0.0 copy-start
  140.0 10.5 %fusion.6 = f32[512,7168]{1,0:T(8,128)} fusion(bf16[512,512]{1,0:T(8,128)(2,1)S(1)} %fusion.1, bf16[7168,512]{1,0:T(8,128)(2,1)} %param.10), kind=kOutput, calls=%fused_computation.19 | convolution fusion | flops 3758096384 | bytes 22544384 | tf_op jit(solution)/shard_map/dot_general | solution.py:30
  150.5 0.0 copy-done
  150.5 0.0 copy-start.1
  150.5 0.0 reduce-scatter.2.cloned.1.call-update
  150.6 0.0 all-gather.7.cloned.1.call-start
  150.6 239.5 %reduce-scatter.2.cloned.1.call-done = f32[64,7168]{1,0:T(8,128)} async-done(((f32[512,7168]{1,0:T(8,128)}), f32[64,7168]{1,0:T(8,128)}) %reduce-scatter.2.cloned.1.call-update) | async-done | bytes 1835024 | tf_op jit(solution)/shard_map/reduce_scatter | solution.py:29
  390.1 0.0 copy-done.1
  390.1 2.9 subtract_convert_fusion
  393.0 0.0 all-gather.7.cloned.1.call-update
  393.0 6.6 %copy.21 = bf16[64,4,8,1792]{3,2,0,1:T(8,128)(2,1)} copy(bf16[64,4,8,1792]{3,2,1,0:T(8,128)(2,1)} %bitcast.30) | data formatting | bytes 14680064 | tf_op jit(solution)/shard_map/all_to_all | solution.py:43
  399.6 5.7 all-to-all-start
  405.3 0.0 all-gather.9.cloned.1.call-start
  405.4 98.4 %all-gather.7.cloned.1.call-done = bf16[512,7168]{1,0:T(8,128)(2,1)} async-done(((bf16[64,7168]{1,0:T(8,128)(2,1)}), bf16[512,7168]{1,0:T(8,128)(2,1)}) %all-gather.7.cloned.1.call-update) | async-done | bytes 7340048 | tf_op jit(solution)/shard_map/all_gather | solution.py:39
  503.8 9.9 %fusion.2 = bf16[512,512]{1,0:T(8,128)(2,1)} fusion(pred[512,512]{1,0:T(32,128)(4,1)S(1)} %reshape.19, bf16[512,7168]{1,0:T(8,128)(2,1)} %all-gather.7.cloned.1.call-done, bf16[7168,512]{1,0:T(8,128)(2,1)} %param.10), kind=kOutput, calls=%fused_computation.9 | convolution fusion | flops 3758620672 | bytes 15466496 | tf_op jit(solution)/shard_map/dot_general | solution.py:40
  513.7 0.0 all-gather.9.cloned.1.call-update
  513.7 6.6 %copy.20 = bf16[64,4,8,1792]{3,2,0,1:T(8,128)(2,1)} copy(bf16[64,4,8,1792]{3,2,1,0:T(8,128)(2,1)} %bitcast.31) | data formatting | bytes 14680064 | tf_op jit(solution)/shard_map/all_to_all | solution.py:44
  520.3 0.0 all-to-all-done
  520.3 5.4 all-to-all-start.1
  525.8 0.2 all-gather.11.cloned.1.call-start
  526.0 0.4 all-gather.11.cloned.1.call-update
  526.4 12.4 %all-gather.9.cloned.1.call-done = bf16[2048,512]{1,0:T(8,128)(2,1)} async-done(((bf16[512,512]{1,0:T(8,128)(2,1)}), bf16[2048,512]{1,0:T(8,128)(2,1)}) %all-gather.9.cloned.1.call-update) | async-done | bytes 2097168 | tf_op jit(solution)/shard_map/all_gather | solution.py:47
  538.8 9.6 %convolution_bitcast_fusion = f32[1792,512]{0,1:T(8,128)} fusion(bf16[2048,512]{1,0:T(8,128)(2,1)} %all-gather.9.cloned.1.call-done, bf16[2048,1792]{1,0:T(8,128)(2,1)} %bitcast.2), kind=kOutput, calls=%fused_computation.3 | convolution fusion | flops 3758096384 | bytes 13107200 | tf_op jit(solution)/shard_map/dot_general | solution.py:8
  548.4 5.2 copy.15
  553.6 23.4 %all-gather.11.cloned.1.call-done = bf16[2048,512]{1,0:T(8,128)(2,1)} async-done(((bf16[512,512]{1,0:T(8,128)(2,1)}), bf16[2048,512]{1,0:T(8,128)(2,1)}) %all-gather.11.cloned.1.call-update) | async-done | bytes 2097168 | tf_op jit(solution)/shard_map/all_gather | solution.py:48
  577.0 46.0 %all-to-all-done.1 = bf16[512,4,1792]{2,0,1:T(8,128)(2,1)} async-done(((bf16[512,4,1792]{2,0,1:T(8,128)(2,1)}), bf16[512,4,1792]{2,0,1:T(8,128)(2,1)}, u32[]{:S(2)}, u32[]{:S(2)}) %all-to-all-start.1) | async-done | bytes 7340064 | tf_op jit(solution)/shard_map/all_to_all | solution.py:44
  623.1 9.5 %fusion.7 = f32[1792,512]{1,0:T(8,128)} fusion(bf16[2048,1792]{1,0:T(8,128)(2,1)} %bitcast.5, bf16[2048,512]{1,0:T(8,128)(2,1)} %all-gather.11.cloned.1.call-done), kind=kOutput, calls=%fused_computation.20 | convolution fusion | flops 3758096384 | bytes 13107200 | tf_op jit(solution)/shard_map/dot_general | solution.py:8
  (3 shorter events, 0.0 us)
Async XLA Ops:
  7.2 123.7 %all-gather.5.cloned.1.call-start = ((), (), s32[]{:S(2)}) async-start(), calls=%async_computation.3 | async-start | bytes 8257536 | tf_op jit(solution)/shard_map/all_gather | solution.py:19
  7.9 382.2 %reduce-scatter.2.cloned.1.call-start = ((), (), s32[]{:S(2)}) async-start(), calls=%async_computation.4 | async-start | bytes 16515072 | tf_op jit(solution)/shard_map/reduce_scatter | solution.py:29
  140.0 10.5 %copy-start = (bf16[512,512]{1,0:T(8,128)(2,1)}, bf16[512,512]{1,0:T(8,128)(2,1)S(1)}, u32[]{:S(2)}) copy-start(bf16[512,512]{1,0:T(8,128)(2,1)S(1)} %fusion.1) | copy-start | bytes 1572868
  150.5 239.6 %copy-start.1 = (f32[7168]{0:T(1024)S(1)}, f32[7168]{0:T(1024)}, u32[]{:S(2)}) copy-start(f32[7168]{0:T(1024)} %param.11) | copy-start | bytes 86020
  150.6 353.2 %all-gather.7.cloned.1.call-start = ((), (), s32[]{:S(2)}) async-start(), calls=%async_computation.5 | async-start | bytes 8257536 | tf_op jit(solution)/shard_map/all_gather | solution.py:39
  399.6 120.8 %all-to-all-start = ((bf16[512,4,1792]{2,0,1:T(8,128)(2,1)}), bf16[512,4,1792]{2,0,1:T(8,128)(2,1)}, u32[]{:S(2)}, u32[]{:S(2)}) async-start(bf16[512,4,1792]{2,0,1:T(8,128)(2,1)} %bitcast.29), calls=%async_computation.1 | async-start | bytes 14680064 | tf_op jit(solution)/shard_map/all_to_all | solution.py:43
  405.3 133.5 %all-gather.9.cloned.1.call-start = ((), (), s32[]{:S(2)}) async-start(), calls=%async_computation.6 | async-start | bytes 2621440 | tf_op jit(solution)/shard_map/all_gather | solution.py:47
  520.3 102.7 %all-to-all-start.1 = ((bf16[512,4,1792]{2,0,1:T(8,128)(2,1)}), bf16[512,4,1792]{2,0,1:T(8,128)(2,1)}, u32[]{:S(2)}, u32[]{:S(2)}) async-start(bf16[512,4,1792]{2,0,1:T(8,128)(2,1)} %bitcast.28), calls=%async_computation.2 | async-start | bytes 14680064 | tf_op jit(solution)/shard_map/all_to_all | solution.py:44
  525.8 51.2 %all-gather.11.cloned.1.call-start = ((), (), s32[]{:S(2)}) async-start(), calls=%async_computation.7 | async-start | bytes 2621440 | tf_op jit(solution)/shard_map/all_gather | solution.py:48
Sparse Core Ops, SparseCore 0:
  10.2 113.9 all-gather.4
  150.7 239.3 reduce-scatter.1
  393.1 110.5 all-gather.6
  513.8 24.9 all-gather.8
  540.2 36.7 all-gather.10
where the time goes:
time: 640 us; the launch traced here: 639 us
  waiting for transfers between devices  421 us (66%)
  local copies, waits for them, and re-layouts  139 us (22%)
  matrix products  48.7 us (8%)
  between operations  13.9 us (2%)
  starting transfers between devices  11.5 us (2%)
    reduce_scatter x1, waiting for transfers between devices, body(): lax.psum_scatter(lax.dot_general(codes, decoder_weight, (((1,), (1,)), ((...  240 us
    unnamed x9, local copies, waits for them, and re-layouts  126 us
    all_gather x1, waiting for transfers between devices, body(): error = lax.all_gather(error_rows, 'feat', axis=0, tiled=True)  98.4 us
    all_to_all x1, waiting for transfers between devices, body(): lax.all_to_all(error, 'tok', split_axis=1, concat_axis=0, tiled=True)  46 us
    all_gather x1, waiting for transfers between devices, body(): lax.all_gather(codes, 'tok', axis=0, tiled=True)  23.4 us
    dot_general x2, matrix products, contract_rows(): lax.dot_general(left, right, (((0,), (0,)), ((), ())), preferred_element_...  19.1 us
  transfers between devices with their start and end apart: 7, of which 5 were waited for; matrix products, arithmetic and copies ran while one was open for 25% of the time, Pallas kernels for 0%

commit v1 on v0

--- a/solution.py
+++ b/solution.py
@@ -36,7 +36,12 @@
     )
     own_rows = lax.dynamic_slice_in_dim(gathered, owner * row_share, row_share, 0)
     error_rows = (rebuilt + decoder_bias - own_rows.astype(jnp.float32)).astype(jnp.bfloat16)
-    error = lax.all_gather(error_rows, "feat", axis=0, tiled=True)
+    ring = [error_rows]
+    for hop in range(7):
+        ring.append(lax.ppermute(ring[-1], "feat", [(dev, (dev + 1) % 8) for dev in range(8)]))
+    error = jnp.roll(
+        jnp.concatenate(ring[::-1], axis=0), (lax.axis_index("feat") + 1) * ring[0].shape[0], axis=0
+    )
     pulled = jnp.dot(error, decoder_weight, preferred_element_type=jnp.float32)
     code_grads = jnp.where(chosen > 0.0, pulled, 0.0).astype(jnp.bfloat16)
     input_cols, error_cols = (

time: 640 us -> 762 us (1.19)
  waiting for transfers between devices: 421 us -> 497 us
  local copies, waits for them, and re-layouts: 139 us -> 187 us
    ppermute x0 -> x7, waiting for transfers between devices: none -> 142 us  [body(): lax.ppermute(ring[-1], 'feat', [(dev, (dev + 1) % 8) for dev in range(8)])]
    all_gather x1 -> x0, waiting for transfers between devices: 98.4 us -> none  [body(): error = lax.all_gather(error_rows, 'feat', axis=0, tiled=True)]
    all_to_all x1, waiting for transfers between devices: 0.01 us -> 36.7 us  [body(): lax.all_to_all(gathered, 'tok', split_axis=1, concat_axis=0, tiled=True)]
    all_to_all x1, waiting for transfers between devices: 46 us -> 77.7 us  [body(): lax.all_to_all(error, 'tok', split_axis=1, concat_axis=0, tiled=True)]
    unnamed x9 -> x38, local copies, waits for them, and re-layouts: 126 us -> 155 us
    all_gather x1, waiting for transfers between devices: 23.4 us -> 0.01 us  [body(): lax.all_gather(codes, 'tok', axis=0, tiled=True)]
    dynamic_slice x0 -> x2, local copies, waits for them, and re-layouts: none -> 14 us  [body(): jnp.roll(jnp.concatenate(ring[::-1], axis=0), (lax.axis_index('feat') + 1...]
    all_gather x1, waiting for transfers between devices: 12.4 us -> 0.02 us  [body(): lax.all_gather(code_grads, 'tok', axis=0, tiled=True)]
  transfers between devices with their start and end apart: 7 -> 13, of which waited for: 5 -> 10; matrix products, arithmetic and copies ran while one was open for 25% -> 26% of each run, Pallas kernels for 0% -> 0%
where the time goes in v1:
time: 762 us; the launch traced here: 760 us
  waiting for transfers between devices  497 us (65%)
  local copies, waits for them, and re-layouts  187 us (25%)
  matrix products  45.9 us (6%)
  between operations  14 us (2%)
  starting transfers between devices  12.8 us (2%)
    reduce_scatter x1, waiting for transfers between devices, body(): lax.psum_scatter(lax.dot_general(codes, decoder_weight, (((1,), (1,)), ((...  240 us
    unnamed x38, local copies, waits for them, and re-layouts  155 us
    ppermute x7, waiting for transfers between devices, body(): lax.ppermute(ring[-1], 'feat', [(dev, (dev + 1) % 8) for dev in range(8)])  142 us
    all_to_all x1, waiting for transfers between devices, body(): lax.all_to_all(error, 'tok', split_axis=1, concat_axis=0, tiled=True)  77.7 us
    all_to_all x1, waiting for transfers between devices, body(): lax.all_to_all(gathered, 'tok', split_axis=1, concat_axis=0, tiled=True)  36.7 us
    dot_general x2, matrix products, contract_rows(): lax.dot_general(left, right, (((0,), (0,)), ((), ())), preferred_element_...  19.1 us
  transfers between devices with their start and end apart: 13, of which 10 were waited for; matrix products, arithmetic and copies ran while one was open for 26% of the time, Pallas kernels for 0%

profile of v1, /device:TPU:0, one launch (start us, length us, event | category | flops | bytes accessed | tf_op | source)
XLA Modules:
  0.0 760.4 jit_solution(14447818664293799185)
XLA Ops:
  7.2 0.0 all-gather.4.cloned.1.call-start
  7.2 0.7 all-gather.4.cloned.1.call-update
  7.9 0.0 reduce-scatter.2.cloned.1.call-start
  7.9 0.9 fusion.5
  8.9 0.1 and_reduce_fusion
  9.0 0.8 multiply_reduce_fusion
  9.8 0.1 copy.15
  9.9 0.1 reshape.20
  10.0 120.3 %scatter_custom_fusion = f32[262144]{0:T(1024)S(1)} fusion(s32[32768]{0:T(1024)S(1)} %reshape.20, f32[32768]{0:T(1024)S(1)} %broadcast.31, f32[]{:T(128)} %constant.16.clone.1), kind=kCustom, calls=%fused_computation.10 | custom fusion | bytes 1048580
  130.3 0.1 broadcast_compare_fusion
  130.5 0.4 reshape.19
  130.8 0.0 all-gather.4.cloned.1.call-done
  130.9 9.1 %fusion.1 = bf16[512,512]{1,0:T(8,128)(2,1)S(1)} fusion(pred[512,512]{1,0:T(32,128)(4,1)S(1)} %reshape.19, bf16[512,7168]{1,0:T(8,128)(2,1)} %all-gather.4.cloned.1.call-done, bf16[7168,512]{1,0:T(8,128)(2,1)} %param.8, f32[512]{0:T(512)} %param.9), kind=kOutput, calls=%fused_computation.7 | convolution fusion | flops 3758882816 | bytes 15468544 | tf_op jit(solution)/shard_map/dot_general | solution.py:20
  140.0 0.0 copy-start.8
  140.0 10.6 %fusion.6 = f32[512,7168]{1,0:T(8,128)} fusion(bf16[512,512]{1,0:T(8,128)(2,1)S(1)} %fusion.1, bf16[7168,512]{1,0:T(8,128)(2,1)} %param.10), kind=kOutput, calls=%fused_computation.35 | convolution fusion | flops 3758096384 | bytes 22544384 | tf_op jit(solution)/shard_map/dot_general | solution.py:30
  150.6 0.0 reduce-scatter.2.cloned.1.call-update
  150.7 239.5 %reduce-scatter.2.cloned.1.call-done = f32[64,7168]{1,0:T(8,128)} async-done(((f32[512,7168]{1,0:T(8,128)}), f32[64,7168]{1,0:T(8,128)}) %reduce-scatter.2.cloned.1.call-update) | async-done | bytes 1835024 | tf_op jit(solution)/shard_map/reduce_scatter | solution.py:29
  390.2 1.9 subtract_convert_fusion
  392.1 1.5 collective-permute-start
  393.6 23.2 %collective-permute-done = bf16[64,7168]{1,0:T(8,128)(2,1)S(1)} collective-permute-done((bf16[64,7168]{1,0:T(8,128)(2,1)S(1)}, bf16[64,7168]{1,0:T(8,128)(2,1)S(1)}, u32[]{:S(2)}, u32[]{:S(2)}) %collective-permute-start) | collective-permute-done | bytes 917536 | tf_op jit(solution)/shard_map/ppermute | solution.py:41
  416.9 23.9 %collective-permute-done.1 = bf16[64,7168]{1,0:T(8,128)(2,1)S(1)} collective-permute-done((bf16[64,7168]{1,0:T(8,128)(2,1)S(1)}, bf16[64,7168]{1,0:T(8,128)(2,1)S(1)}, u32[]{:S(2)}, u32[]{:S(2)}) %collective-permute-start.1) | collective-permute-done | bytes 917536 | tf_op jit(solution)/shard_map/ppermute | solution.py:41
  440.8 23.0 %collective-permute-done.2 = bf16[64,7168]{1,0:T(8,128)(2,1)S(1)} collective-permute-done((bf16[64,7168]{1,0:T(8,128)(2,1)S(1)}, bf16[64,7168]{1,0:T(8,128)(2,1)S(1)}, u32[]{:S(2)}, u32[]{:S(2)}) %collective-permute-start.2) | collective-permute-done | bytes 917536 | tf_op jit(solution)/shard_map/ppermute | solution.py:41
  463.8 1.0 copy-done.1
  464.8 22.1 %collective-permute-done.3 = bf16[64,7168]{1,0:T(8,128)(2,1)S(1)} collective-permute-done((bf16[64,7168]{1,0:T(8,128)(2,1)S(1)}, bf16[64,7168]{1,0:T(8,128)(2,1)S(1)}, u32[]{:S(2)}, u32[]{:S(2)}) %collective-permute-start.3) | collective-permute-done | bytes 917536 | tf_op jit(solution)/shard_map/ppermute | solution.py:41
  486.9 0.9 copy-done.3
  487.8 21.3 %collective-permute-done.4 = bf16[64,7168]{1,0:T(8,128)(2,1)S(1)} collective-permute-done((bf16[64,7168]{1,0:T(8,128)(2,1)S(1)}, bf16[64,7168]{1,0:T(8,128)(2,1)S(1)}, u32[]{:S(2)}, u32[]{:S(2)}) %collective-permute-start.4) | collective-permute-done | bytes 917536 | tf_op jit(solution)/shard_map/ppermute | solution.py:41
  509.1 0.9 copy-done.5
  510.0 20.5 %collective-permute-done.5 = bf16[64,7168]{1,0:T(8,128)(2,1)} collective-permute-done((bf16[64,7168]{1,0:T(8,128)(2,1)S(1)}, bf16[64,7168]{1,0:T(8,128)(2,1)}, u32[]{:S(2)}, u32[]{:S(2)}) %collective-permute-start.5) | collective-permute-done | bytes 917536 | tf_op jit(solution)/shard_map/ppermute | solution.py:41
  530.6 6.5 copy.22
  537.1 5.4 all-to-all-start
  542.5 0.0 all-gather.6.cloned.1.call-start
  542.6 0.0 copy-start.4
  542.6 7.9 %collective-permute-done.6 = bf16[64,7168]{1,0:T(8,128)(2,1)} collective-permute-done((bf16[64,7168]{1,0:T(8,128)(2,1)}, bf16[64,7168]{1,0:T(8,128)(2,1)}, u32[]{:S(2)}, u32[]{:S(2)}) %collective-permute-start.6) | collective-permute-done | bytes 917536 | tf_op jit(solution)/shard_map/ppermute | solution.py:41
  550.5 2.2 constant_dynamic-update-slice_fusion.15
  552.6 2.2 constant_dynamic-update-slice_fusion.14
  554.9 2.2 constant_dynamic-update-slice_fusion.13
  557.0 2.2 constant_dynamic-update-slice_fusion.12
  559.2 2.2 constant_dynamic-update-slice_fusion.11
  561.4 1.0 constant_dynamic-update-slice_fusion.10
  562.4 1.0 constant_dynamic-update-slice_fusion.9
  563.4 1.0 constant_dynamic-update-slice_fusion.8
  564.4 2.2 constant_dynamic-update-slice_fusion.7
  566.6 2.2 constant_dynamic-update-slice_fusion.6
  568.8 1.0 constant_dynamic-update-slice_fusion.5
  569.8 1.0 constant_dynamic-update-slice_fusion.4
  570.8 1.0 constant_dynamic-update-slice_fusion.3
  571.8 1.0 constant_dynamic-update-slice_fusion.2
  572.8 1.0 constant_dynamic-update-slice_fusion.1
  573.8 1.0 constant_dynamic-update-slice_fusion
  574.8 3.6 constant_dynamic-slice_fusion
  578.4 3.0 copy-done
  581.4 7.1 fusion.2
  588.5 0.0 all-gather.6.cloned.1.call-update
  588.5 10.5 %copy.17 = bf16[512,7168]{0,1:T(8,128)(2,1)} copy(bf16[512,7168]{1,0:T(8,128)(2,1)} %copy-done) | data formatting | bytes 14680064 | tf_op jit(solution)/shard_map/jit(_roll_dynamic)/dynamic_slice | solution.py:42
  599.0 36.7 %all-to-all-done = bf16[512,4,1792]{2,0,1:T(8,128)(2,1)} async-done(((bf16[512,4,1792]{2,0,1:T(8,128)(2,1)}), bf16[512,4,1792]{2,0,1:T(8,128)(2,1)}, u32[]{:S(2)}, u32[]{:S(2)}) %all-to-all-start) | async-done | bytes 7340064 | tf_op jit(solution)/shard_map/all_to_all | solution.py:48
  635.7 5.5 all-to-all-start.1
  641.2 0.2 all-gather.8.cloned.1.call-start
  641.4 0.3 all-gather.8.cloned.1.call-update
  641.7 0.0 all-gather.6.cloned.1.call-done
  641.8 9.6 %convolution_bitcast_fusion = f32[1792,512]{0,1:T(8,128)} fusion(bf16[2048,512]{1,0:T(8,128)(2,1)} %all-gather.6.cloned.1.call-done, bf16[2048,1792]{1,0:T(8,128)(2,1)} %bitcast.2), kind=kOutput, calls=%fused_computation.2 | convolution fusion | flops 3758096384 | bytes 13107200 | tf_op jit(solution)/shard_map/dot_general | solution.py:8
  651.4 5.2 copy.19
  656.6 77.7 %all-to-all-done.1 = bf16[512,4,1792]{0,2,1:T(8,128)(2,1)} async-done(((bf16[512,4,1792]{0,2,1:T(8,128)(2,1)}), bf16[512,4,1792]{0,2,1:T(8,128)(2,1)}, u32[]{:S(2)}, u32[]{:S(2)}) %all-to-all-start.1) | async-done | bytes 7340064 | tf_op jit(solution)/shard_map/all_to_all | solution.py:49
  734.3 10.0 %copy.18 = bf16[4,512,1792]{2,1,0:T(8,128)(2,1)} copy(bf16[4,512,1792]{1,2,0:T(8,128)(2,1)} %bitcast.5) | data formatting | bytes 14680064 | tf_op jit(solution)/shard_map/all_to_all | solution.py:49
  744.3 9.5 %fusion.7 = f32[1792,512]{1,0:T(8,128)} fusion(bf16[2048,1792]{1,0:T(8,128)(2,1)} %bitcast.27, bf16[2048,512]{1,0:T(8,128)(2,1)} %all-gather.8.cloned.1.call-done), kind=kOutput, calls=%fused_computation.36 | convolution fusion | flops 3758096384 | bytes 13107200 | tf_op jit(solution)/shard_map/dot_general | solution.py:8
  (22 shorter events, 0.1 us)
Async XLA Ops:
  7.2 123.7 %all-gather.4.cloned.1.call-start = ((), (), s32[]{:S(2)}) async-start(), calls=%async_computation.3 | async-start | bytes 8257536 | tf_op jit(solution)/shard_map/all_gather | solution.py:19
  7.9 382.3 %reduce-scatter.2.cloned.1.call-start = ((), (), s32[]{:S(2)}) async-start(), calls=%async_computation.4 | async-start | bytes 16515072 | tf_op jit(solution)/shard_map/reduce_scatter | solution.py:29
  140.0 10.6 %copy-start.7 = (bf16[512,512]{1,0:T(8,128)(2,1)}, bf16[512,512]{1,0:T(8,128)(2,1)S(1)}, u32[]{:S(2)}) copy-start(bf16[512,512]{1,0:T(8,128)(2,1)S(1)} %fusion.1) | copy-start | bytes 1572868
  140.0 250.2 %copy-start.8 = (f32[7168]{0:T(1024)S(1)}, f32[7168]{0:T(1024)}, u32[]{:S(2)}) copy-start(f32[7168]{0:T(1024)} %param.11) | copy-start | bytes 86020
  392.1 24.8 %collective-permute-start = (bf16[64,7168]{1,0:T(8,128)(2,1)S(1)}, bf16[64,7168]{1,0:T(8,128)(2,1)S(1)}, u32[]{:S(2)}, u32[]{:S(2)}) collective-permute-start(bf16[64,7168]{1,0:T(8,128)(2,1)S(1)} %subtract_convert_fusion), channel_id=1, source_target_pairs={{0,4},{4,8},{8,12},{12,16},{16,20},{20,24},{24,28},{28,0},{1,5},{5... | collective-permute-start | bytes 2752520 | tf_op jit(solution)/shard_map/ppermute | solution.py:41
  416.9 23.9 %collective-permute-start.1 = (bf16[64,7168]{1,0:T(8,128)(2,1)S(1)}, bf16[64,7168]{1,0:T(8,128)(2,1)S(1)}, u32[]{:S(2)}, u32[]{:S(2)}) collective-permute-start(bf16[64,7168]{1,0:T(8,128)(2,1)S(1)} %collective-permute-done), channel_id=1, source_target_pairs={{0,4},{4,8},{8,12},{12,16},{16,20},{20,24},{24,28},{28,0},{1,5},{5... | collective-permute-start | bytes 2752520 | tf_op jit(solution)/shard_map/ppermute | solution.py:41
  440.8 23.0 %collective-permute-start.2 = (bf16[64,7168]{1,0:T(8,128)(2,1)S(1)}, bf16[64,7168]{1,0:T(8,128)(2,1)S(1)}, u32[]{:S(2)}, u32[]{:S(2)}) collective-permute-start(bf16[64,7168]{1,0:T(8,128)(2,1)S(1)} %collective-permute-done.1), channel_id=1, source_target_pairs={{0,4},{4,8},{8,12},{12,16},{16,20},{20,24},{24,28},{28,0},{1,5},{5... | collective-permute-start | bytes 2752520 | tf_op jit(solution)/shard_map/ppermute | solution.py:41
  463.8 1.0 copy-start.1
  464.8 22.1 %collective-permute-start.3 = (bf16[64,7168]{1,0:T(8,128)(2,1)S(1)}, bf16[64,7168]{1,0:T(8,128)(2,1)S(1)}, u32[]{:S(2)}, u32[]{:S(2)}) collective-permute-start(bf16[64,7168]{1,0:T(8,128)(2,1)S(1)} %collective-permute-done.2), channel_id=1, source_target_pairs={{0,4},{4,8},{8,12},{12,16},{16,20},{20,24},{24,28},{28,0},{1,5},{5... | collective-permute-start | bytes 2752520 | tf_op jit(solution)/shard_map/ppermute | solution.py:41
  486.9 0.9 copy-start.3
  487.8 21.3 %collective-permute-start.4 = (bf16[64,7168]{1,0:T(8,128)(2,1)S(1)}, bf16[64,7168]{1,0:T(8,128)(2,1)S(1)}, u32[]{:S(2)}, u32[]{:S(2)}) collective-permute-start(bf16[64,7168]{1,0:T(8,128)(2,1)S(1)} %collective-permute-done.3), channel_id=1, source_target_pairs={{0,4},{4,8},{8,12},{12,16},{16,20},{20,24},{24,28},{28,0},{1,5},{5... | collective-permute-start | bytes 2752520 | tf_op jit(solution)/shard_map/ppermute | solution.py:41
  509.1 0.9 copy-start.5
  510.0 20.5 %collective-permute-start.5 = (bf16[64,7168]{1,0:T(8,128)(2,1)S(1)}, bf16[64,7168]{1,0:T(8,128)(2,1)}, u32[]{:S(2)}, u32[]{:S(2)}) collective-permute-start(bf16[64,7168]{1,0:T(8,128)(2,1)S(1)} %collective-permute-done.4), channel_id=1, source_target_pairs={{0,4},{4,8},{8,12},{12,16},{16,20},{20,24},{24,28},{28,0},{1,5},{5... | collective-permute-start | bytes 2752520 | tf_op jit(solution)/shard_map/ppermute | solution.py:41
  530.6 19.9 %collective-permute-start.6 = (bf16[64,7168]{1,0:T(8,128)(2,1)}, bf16[64,7168]{1,0:T(8,128)(2,1)}, u32[]{:S(2)}, u32[]{:S(2)}) collective-permute-start(bf16[64,7168]{1,0:T(8,128)(2,1)} %collective-permute-done.5), channel_id=1, source_target_pairs={{0,4},{4,8},{8,12},{12,16},{16,20},{20,24},{24,28},{28,0},{1,5},{5... | collective-permute-start | bytes 2752520 | tf_op jit(solution)/shard_map/ppermute | solution.py:41
  537.1 98.6 %all-to-all-start = ((bf16[512,4,1792]{2,0,1:T(8,128)(2,1)}), bf16[512,4,1792]{2,0,1:T(8,128)(2,1)}, u32[]{:S(2)}, u32[]{:S(2)}) async-start(bf16[512,4,1792]{2,0,1:T(8,128)(2,1)} %bitcast.24), calls=%async_computation.1 | async-start | bytes 14680064 | tf_op jit(solution)/shard_map/all_to_all | solution.py:48
  542.5 99.2 %all-gather.6.cloned.1.call-start = ((), (), s32[]{:S(2)}) async-start(), calls=%async_computation.5 | async-start | bytes 2621440 | tf_op jit(solution)/shard_map/all_gather | solution.py:52
  542.6 26.3 %copy-start.6 = (bf16[64,7168]{1,0:T(8,128)(2,1)S(1)}, bf16[64,7168]{1,0:T(8,128)(2,1)}, u32[]{:S(2)}) copy-start(bf16[64,7168]{1,0:T(8,128)(2,1)} %copy-done.5) | copy-start | bytes 2752516
  542.6 27.2 %copy-start.4 = (bf16[64,7168]{1,0:T(8,128)(2,1)S(1)}, bf16[64,7168]{1,0:T(8,128)(2,1)}, u32[]{:S(2)}) copy-start(bf16[64,7168]{1,0:T(8,128)(2,1)} %copy-done.3) | copy-start | bytes 2752516
  542.6 28.2 %copy-start.2 = (bf16[64,7168]{1,0:T(8,128)(2,1)S(1)}, bf16[64,7168]{1,0:T(8,128)(2,1)}, u32[]{:S(2)}) copy-start(bf16[64,7168]{1,0:T(8,128)(2,1)} %copy-done.1) | copy-start | bytes 2752516
  578.4 3.0 copy-start
  635.7 98.6 %all-to-all-start.1 = ((bf16[512,4,1792]{0,2,1:T(8,128)(2,1)}), bf16[512,4,1792]{0,2,1:T(8,128)(2,1)}, u32[]{:S(2)}, u32[]{:S(2)}) async-start(bf16[512,4,1792]{0,2,1:T(8,128)(2,1)} %bitcast.25), calls=%async_computation.2 | async-start | bytes 14680064 | tf_op jit(solution)/shard_map/all_to_all | solution.py:49
  641.2 103.1 %all-gather.8.cloned.1.call-start = ((), (), s32[]{:S(2)}) async-start(), calls=%async_computation.6 | async-start | bytes 2621440 | tf_op jit(solution)/shard_map/all_gather | solution.py:53
Sparse Core Ops, SparseCore 0:
  10.2 113.9 all-gather.3
  150.8 239.3 reduce-scatter.1
  588.6 31.2 all-gather.5
  643.2 35.7 all-gather.7
